TPU v7x, 32 devices: a whole 2x2x4 slice. The times are simulated.
32 devices in a mesh: samp: 16 (over z, x, core), var: 2 (over y).
Axes of the slice: x: 2, y: 2, z: 4, core: 2. Of those that a mesh axis runs over, the one named last changes fastest.
Arguments:
- genotypes: bfloat16 [16384, 12288], P('samp', 'var'), may hold values from 0 to 2, as said below
- start_q: float32 [64, 16384], P(None, 'samp'), may hold values from 0 to 1, as said below
Outputs:
- final_q: float32 [64, 16384], P(None, 'samp')
- final_p: float32 [64, 12288], P(None, 'var')
Inputs may be any that keep to these rules, and one draw needn't show every extreme that they name: `genotypes`: genotype counts, whole numbers. `start_q`: nonnegative proportions.
All inputs are finite; a program needn't handle non-finite values.
Results may differ from a plain program's by a relative error of at most 0.001.
Values sent between devices are 32-bit elements; how exact they have to be, the bound alone decides.
No kernel may reach another device: no remote copies, remote signals or barrier semaphores. Data moves between devices by JAX's collectives and lax.ppermute only.
A program may use at most 64 MiB of HBM per device.

v0:
```python
import jax
import jax.numpy as jnp
from jax import lax
from jax.sharding import PartitionSpec as P

ITERS = 2
ridge_term = 1.0


def gram_solve(gram_matrix, right_side):
    eye_matrix = jnp.eye(gram_matrix.shape[0], dtype=jnp.float32)
    factor_low = jnp.linalg.cholesky(gram_matrix + ridge_term * eye_matrix)
    return jax.scipy.linalg.cho_solve((factor_low, True), right_side)


def body(genotypes, start_q):
    halved = genotypes * jnp.asarray(0.5, dtype=genotypes.dtype)
    ancestry = start_q
    frequency = None
    for iteration in range(ITERS):
        ancestry_b = ancestry.astype(jnp.bfloat16)
        cross_part = jnp.dot(ancestry_b, halved, preferred_element_type=jnp.float32)
        gram_part = jnp.dot(ancestry, ancestry.T, precision=lax.Precision.HIGHEST)
        width = cross_part.shape[1]
        summed = lax.psum(jnp.concatenate([cross_part, gram_part], axis=1), "samp")
        frequency = gram_solve(summed[:, width:], summed[:, :width])
        freq_b = frequency.astype(jnp.bfloat16)
        sample_part = lax.dot_general(
            freq_b, halved, (((1,), (1,)), ((), ())), preferred_element_type=jnp.float32
        )
        pgram_part = jnp.dot(frequency, frequency.T, precision=lax.Precision.HIGHEST)
        sample_share = lax.psum_scatter(sample_part, "var", scatter_dimension=1, tiled=True)
        gram_p = lax.psum(pgram_part, "var")
        ancestry_share = gram_solve(gram_p, sample_share)
        ancestry = lax.all_gather(ancestry_share, "var", axis=1, tiled=True)
    return (ancestry, frequency)


def solution(mesh):
    return jax.shard_map(
        body,
        mesh=mesh,
        in_specs=(P("samp", "var"), P(None, "samp")),
        out_specs=(P(None, "samp"), P(None, "var")),
        check_vma=False,
    )
```

profile of v0, /device:TPU:0, one launch (start us, length us, event | category | flops | bytes accessed | tf_op | source)
XLA Modules:
  0.0 362.6 jit_solution(11005803779710166309)
XLA Ops:
  7.2 0.0 all-reduce.3.cloned.1.call-start
  7.2 1.4 fusion.55
  8.7 6.6 %fusion.8 = f32[64,6144]{0,1:T(8,128)S(1)} fusion(bf16[1024,6144]{1,0:T(8,128)(2,1)} %param.7, f32[64,1024]{1,0:T(8,128)} %param.8), kind=kOutput, calls=%fused_computation.8 | convolution fusion | flops 811663360 | bytes 14417920 | tf_op jit(solution)/shard_map/dot_general | solution.py:22
  15.3 1.9 pad_maximum_fusion
  17.1 0.0 all-reduce.3.cloned.1.call-update
  17.2 0.2 reduce-scatter.3.cloned.1.call-start
  17.4 106.9 %all-reduce.3.cloned.1.call-done = f32[64,6208]{0,1:T(8,128)} async-done(((f32[64,6208]{0,1:T(8,128)}), f32[64,6208]{0,1:T(8,128)}) %all-reduce.3.cloned.1.call-update) | async-done | bytes 1589264 | tf_op jit(solution)/shard_map/psum | solution.py:25
  124.3 0.8 convert_add_fusion.3
  125.1 0.1 copy.6
  125.1 0.8 fusion.44
  125.9 5.8 %cholesky.74 = f32[64,64]{1,0:T(8,128)S(1)} custom-call(f32[64,64]{1,0:T(8,128)S(1)} %fusion.44), custom_call_target="Cholesky" | custom-call | tf_op jit(solution)/shard_map/jit(cholesky)/cholesky | solution.py:12
  131.8 0.6 compare_reduce_fusion.3
  132.4 0.7 fusion.23
  133.1 4.9 %custom-call.14 = f32[1,64,64]{1,2,0:T(8,128)S(1)} custom-call(f32[1,64,64]{2,1,0:T(8,128)S(1)} %fusion.23), custom_call_target="InvertDiagBlocksLowerTriangular" | custom-call | tf_op jit(solution)/shard_map/jit(_cho_solve)/triangular_solve | solution.py:13
  138.0 5.3 %fusion.17 = f32[64,6144]{1,0:T(8,128)S(1)} fusion(f32[64,6208]{0,1:T(8,128)} %all-reduce.3.cloned.1.call-done, f32[1,64,64]{1,2,0:T(8,128)S(1)} %custom-call.14), kind=kOutput, calls=%fused_computation.17 | convolution fusion | flops 301989888 | bytes 4734976 | tf_op jit(solution)/shard_map/jit(_cho_solve)/triangular_solve | solution.py:13
  143.3 1.5 fusion.41
  144.8 1.4 fusion.56
  146.2 9.2 %fusion.4 = f32[64,1024]{1,0:T(8,128)} fusion(bf16[1024,6144]{1,0:T(8,128)(2,1)} %param.7, f32[64,6144]{1,0:T(8,128)S(1)} %fusion.41), kind=kOutput, calls=%fused_computation.4 | convolution fusion | flops 811991040 | bytes 14417920 | tf_op jit(solution)/shard_map/dot_general | solution.py:28
  155.4 8.3 %psum.29 = f32[64,64]{0,1:T(8,128)S(1)} all-reduce(f32[64,64]{0,1:T(8,128)S(1)} %fusion.56), channel_id=1, replica_groups=mesh['samp'=16,'var'=2] {'var'}, use_global_device_ids=true, to_apply=%region_3.6 | all-reduce | flops 4096 | bytes 32768 | tf_op jit(solution)/shard_map/psum | solution.py:33
  163.7 0.0 reduce-scatter.3.cloned.1.call-update
  163.7 0.3 all-reduce.5.cloned.1.call-start
  164.0 0.1 copy.8
  164.1 5.8 %cholesky.85 = f32[64,64]{1,0:T(8,128)S(1)} custom-call(f32[64,64]{1,0:T(8,128)S(1)} %fusion.40), custom_call_target="Cholesky" | custom-call | tf_op jit(solution)/shard_map/jit(cholesky)/cholesky | solution.py:12
  170.0 0.6 compare_reduce_fusion.2
  170.7 0.7 fusion.24
  171.3 4.9 %custom-call.15 = f32[1,64,64]{1,2,0:T(8,128)S(1)} custom-call(f32[1,64,64]{2,1,0:T(8,128)S(1)} %fusion.24), custom_call_target="InvertDiagBlocksLowerTriangular" | custom-call | tf_op jit(solution)/shard_map/jit(_cho_solve)/triangular_solve | solution.py:13
  176.2 0.0 reduce-scatter.3.cloned.1.call-done
  176.2 1.2 fusion.38
  177.5 0.3 fusion.36
  177.7 5.6 %all_gather.6 = f32[64,1024]{1,0:T(8,128)S(1)} all-gather(f32[64,512]{1,0:T(8,128)S(1)} %fusion.36), channel_id=1, replica_groups=mesh['samp'=16,'var'=2] {'var'}, dimensions={1}, use_global_device_ids=true | all-gather | bytes 393216 | tf_op jit(solution)/shard_map/all_gather | solution.py:35
  183.4 0.4 fusion.57
  183.8 8.0 %fusion.2 = f32[64,6144]{0,1:T(8,128)S(1)} fusion(bf16[1024,6144]{1,0:T(8,128)(2,1)} %param.7, f32[64,1024]{1,0:T(8,128)S(1)} %all_gather.6), kind=kOutput, calls=%fused_computation.2 | convolution fusion | flops 811663360 | bytes 14417920 | tf_op jit(solution)/shard_map/dot_general | solution.py:22
  191.7 1.9 pad_maximum_fusion.1
  193.6 0.0 all-reduce.5.cloned.1.call-update
  193.6 0.0 reduce-scatter.5.cloned.1.call-start
  193.7 103.0 %all-reduce.5.cloned.1.call-done = f32[64,6208]{0,1:T(8,128)} async-done(((f32[64,6208]{0,1:T(8,128)}), f32[64,6208]{0,1:T(8,128)}) %all-reduce.5.cloned.1.call-update) | async-done | bytes 1589264 | tf_op jit(solution)/shard_map/psum | solution.py:25
  296.6 0.8 convert_add_fusion.1
  297.4 0.1 copy.11
  297.5 0.8 fusion.35
  298.3 5.8 %cholesky.96 = f32[64,64]{1,0:T(8,128)S(1)} custom-call(f32[64,64]{1,0:T(8,128)S(1)} %fusion.35), custom_call_target="Cholesky" | custom-call | tf_op jit(solution)/shard_map/jit(cholesky)/cholesky | solution.py:12
  304.1 0.6 compare_reduce_fusion.1
  304.8 0.7 fusion.25
  305.4 4.9 %custom-call.16 = f32[1,64,64]{1,2,0:T(8,128)S(1)} custom-call(f32[1,64,64]{2,1,0:T(8,128)S(1)} %fusion.25), custom_call_target="InvertDiagBlocksLowerTriangular" | custom-call | tf_op jit(solution)/shard_map/jit(_cho_solve)/triangular_solve | solution.py:13
  310.3 5.3 %fusion.15 = f32[64,6144]{1,0:T(8,128)S(1)} fusion(f32[64,6208]{0,1:T(8,128)} %all-reduce.5.cloned.1.call-done, f32[1,64,64]{1,2,0:T(8,128)S(1)} %custom-call.16), kind=kOutput, calls=%fused_computation.15 | convolution fusion | flops 301989888 | bytes 4734976 | tf_op jit(solution)/shard_map/jit(_cho_solve)/triangular_solve | solution.py:13
  315.7 1.5 fusion.32
  317.2 0.0 copy-start
  317.2 1.4 fusion.58
  318.6 9.2 %fusion = f32[64,1024]{1,0:T(8,128)} fusion(bf16[1024,6144]{1,0:T(8,128)(2,1)} %param.7, f32[64,6144]{1,0:T(8,128)S(1)} %fusion.32), kind=kOutput, calls=%fused_computation | convolution fusion | flops 811991040 | bytes 14417920 | tf_op jit(solution)/shard_map/dot_general | solution.py:28
  327.8 0.0 copy-done
  327.8 8.3 %psum.31 = f32[64,64]{0,1:T(8,128)S(1)} all-reduce(f32[64,64]{0,1:T(8,128)S(1)} %fusion.58), channel_id=1, replica_groups=mesh['samp'=16,'var'=2] {'var'}, use_global_device_ids=true, to_apply=%region_6.10 | all-reduce | flops 4096 | bytes 32768 | tf_op jit(solution)/shard_map/psum | solution.py:33
  336.1 0.1 copy.13
  336.2 0.0 reduce-scatter.5.cloned.1.call-update
  336.2 5.8 %cholesky.107 = f32[64,64]{1,0:T(8,128)S(1)} custom-call(f32[64,64]{1,0:T(8,128)S(1)} %fusion.31), custom_call_target="Cholesky" | custom-call | tf_op jit(solution)/shard_map/jit(cholesky)/cholesky | solution.py:12
  342.1 0.6 compare_reduce_fusion
  342.7 0.6 fusion.26
  343.3 4.9 %custom-call.17 = f32[1,64,64]{1,2,0:T(8,128)S(1)} custom-call(f32[1,64,64]{2,1,0:T(8,128)S(1)} %fusion.26), custom_call_target="InvertDiagBlocksLowerTriangular" | custom-call | tf_op jit(solution)/shard_map/jit(_cho_solve)/triangular_solve | solution.py:13
  348.2 0.0 reduce-scatter.5.cloned.1.call-done
  348.2 1.2 fusion.29
  349.5 0.3 fusion.27
  349.7 5.6 %all_gather.7 = f32[64,1024]{1,0:T(8,128)S(1)} all-gather(f32[64,512]{1,0:T(8,128)S(1)} %fusion.27), channel_id=1, replica_groups=mesh['samp'=16,'var'=2] {'var'}, dimensions={1}, use_global_device_ids=true | all-gather | bytes 393216 | tf_op jit(solution)/shard_map/all_gather | solution.py:35
  355.4 0.7 copy.23
  (8 shorter events, 0.2 us)
Async XLA Ops:
  7.2 117.1 %all-reduce.3.cloned.1.call-start = ((), (), s32[]{:S(2)}) async-start(), calls=%async_computation.2 | async-start | bytes 6356992 | tf_op jit(solution)/shard_map/psum | solution.py:25
  17.2 159.1 %reduce-scatter.3.cloned.1.call-start = ((), (), s32[]{:S(2)}) async-start(), calls=%async_computation.3 | async-start | bytes 393216 | tf_op jit(solution)/shard_map/reduce_scatter | solution.py:32
  163.7 132.9 %all-reduce.5.cloned.1.call-start = ((), (), s32[]{:S(2)}) async-start(), calls=%async_computation.4 | async-start | bytes 6356992 | tf_op jit(solution)/shard_map/psum | solution.py:25
  193.6 154.6 %reduce-scatter.5.cloned.1.call-start = ((), (), s32[]{:S(2)}) async-start(), calls=%async_computation.5 | async-start | bytes 393216 | tf_op jit(solution)/shard_map/reduce_scatter | solution.py:32
  317.2 10.6 %copy-start = (f32[64,6144]{1,0:T(8,128)}, f32[64,6144]{1,0:T(8,128)S(1)}, u32[]{:S(2)}) copy-start(f32[64,6144]{1,0:T(8,128)S(1)} %fusion.32) | copy-start | bytes 4718596
Sparse Core Ops, SparseCore 0:
  17.3 106.9 all-reduce.2
  163.9 10.4 reduce-scatter.2
  193.8 102.8 all-reduce.4
  336.3 10.3 reduce-scatter.4
where the time goes:
time: 363 us
  waiting for transfers between devices  210 us (58%)
  other arithmetic  55.1 us (15%)
  matrix products  54.1 us (15%)
  blocking collectives  27.9 us (8%)
  between operations  14 us (4%)
    psum x2, waiting for transfers between devices, body(): summed = lax.psum(jnp.concatenate([cross_part, gram_part], axis=1), 'samp')  210 us
    another operation x12, other arithmetic, gram_solve(): factor_low = jnp.linalg.cholesky(gram_matrix + ridge_term * eye_matrix)  26.1 us
    another operation x8, other arithmetic, gram_solve(): return jax.scipy.linalg.cho_solve((factor_low, True), right_side)  22.1 us
    dot_general x2, matrix products, body(): lax.dot_general(freq_b, halved, (((1,), (1,)), ((), ())), preferred_eleme...  18.4 us
    psum x2, blocking collectives, body(): gram_p = lax.psum(pgram_part, 'var')  16.6 us
    another operation x8, matrix products, gram_solve(): return jax.scipy.linalg.cho_solve((factor_low, True), right_side)  16.6 us
    dot_general x2, matrix products, body(): cross_part = jnp.dot(ancestry_b, halved, preferred_element_type=jnp.float32)  14.5 us
    all_gather x2, blocking collectives, body(): ancestry = lax.all_gather(ancestry_share, 'var', axis=1, tiled=True)  11.3 us
  transfers between devices with their start and end apart: 4, of which 2 were waited for; matrix products, arithmetic and copies ran while one was open for 7% of the time, Pallas kernels for 0%

commit v1 on v0

--- a/solution.py
+++ b/solution.py
@@ -22,7 +22,9 @@
         cross_part = jnp.dot(ancestry_b, halved, preferred_element_type=jnp.float32)
         gram_part = jnp.dot(ancestry, ancestry.T, precision=lax.Precision.HIGHEST)
         width = cross_part.shape[1]
-        summed = lax.psum(jnp.concatenate([cross_part, gram_part], axis=1), "samp")
+        summed = jnp.sum(
+            lax.all_gather(jnp.concatenate([cross_part, gram_part], axis=1), "samp"), axis=0
+        )
         frequency = gram_solve(summed[:, width:], summed[:, :width])
         freq_b = frequency.astype(jnp.bfloat16)
         sample_part = lax.dot_general(

time: 363 us -> 424 us (1.17)
  waiting for transfers between devices: 210 us -> 264 us
  other arithmetic: 55.1 us -> 70.3 us
  matrix products: 54.1 us -> 46.1 us
    all_gather x0 -> x2, waiting for transfers between devices: none -> 264 us  [body(): lax.all_gather(jnp.concatenate([cross_part, gram_part], axis=1), 'samp')]
    psum x2 -> x0, waiting for transfers between devices: 210 us -> none  [body(): summed = lax.psum(jnp.concatenate([cross_part, gram_part], axis=1), 'samp')]
    reduce_sum x0 -> x2, other arithmetic: none -> 19.4 us  [body(): jnp.sum(lax.all_gather(jnp.concatenate([cross_part, gram_part], axis=1),...]
    another operation x8, matrix products: 16.6 us -> 8.94 us  [gram_solve(): return jax.scipy.linalg.cho_solve((factor_low, True), right_side)]
  transfers between devices with their start and end apart: 4 -> 4, of which waited for: 2 -> 2; matrix products, arithmetic and copies ran while one was open for 7% -> 6% of each run, Pallas kernels for 0% -> 0%
where the time goes in v1:
time: 424 us
  waiting for transfers between devices  264 us (62%)
  other arithmetic  70.3 us (17%)
  matrix products  46.1 us (11%)
  blocking collectives  27.9 us (7%)
  between operations  14.1 us (3%)
    all_gather x2, waiting for transfers between devices, body(): lax.all_gather(jnp.concatenate([cross_part, gram_part], axis=1), 'samp')  264 us
    another operation x12, other arithmetic, gram_solve(): factor_low = jnp.linalg.cholesky(gram_matrix + ridge_term * eye_matrix)  26.1 us
    another operation x8, other arithmetic, gram_solve(): return jax.scipy.linalg.cho_solve((factor_low, True), right_side)  22.1 us
    reduce_sum x2, other arithmetic, body(): jnp.sum(lax.all_gather(jnp.concatenate([cross_part, gram_part], axis=1),...  19.4 us
    dot_general x2, matrix products, body(): lax.dot_general(freq_b, halved, (((1,), (1,)), ((), ())), preferred_eleme...  18.4 us
    psum x2, blocking collectives, body(): gram_p = lax.psum(pgram_part, 'var')  16.6 us
    dot_general x2, matrix products, body(): cross_part = jnp.dot(ancestry_b, halved, preferred_element_type=jnp.float32)  14.2 us
    all_gather x2, blocking collectives, body(): ancestry = lax.all_gather(ancestry_share, 'var', axis=1, tiled=True)  11.3 us
  transfers between devices with their start and end apart: 4, of which 2 were waited for; matrix products, arithmetic and copies ran while one was open for 6% of the time, Pallas kernels for 0%

profile of v1, /device:TPU:0, one launch (start us, length us, event | category | flops | bytes accessed | tf_op | source)
XLA Modules:
  0.0 424.0 jit_solution(12390600945230578623)
XLA Ops:
  7.2 0.0 all-gather.5.cloned.1.call-start
  7.2 1.5 fusion.55
  8.7 7.1 %fusion.8 = f32[64,6144]{1,0:T(8,128)S(1)} fusion(bf16[1024,6144]{1,0:T(8,128)(2,1)} %param.7, f32[64,1024]{1,0:T(8,128)} %param.8), kind=kOutput, calls=%fused_computation.8 | convolution fusion | flops 811663360 | bytes 14417920 | tf_op jit(solution)/shard_map/dot_general | solution.py:22
  15.8 1.3 pad_maximum_fusion
  17.1 0.0 all-gather.5.cloned.1.call-update
  17.1 0.0 reduce-scatter.3.cloned.1.call-start
  17.2 133.8 %all-gather.5.cloned.1.call-done = f32[1024,6208]{1,0:T(8,128)} async-done(((f32[64,6208]{1,0:T(8,128)}), f32[1024,6208]{1,0:T(8,128)}) %all-gather.5.cloned.1.call-update) | async-done | bytes 25427984 | tf_op jit(solution)/shard_map/all_gather | solution.py:26
  151.0 9.7 %reduce_sum.18 = f32[64,6208]{1,0:T(8,128)S(1)} reduce(f32[16,64,6208]{2,1,0:T(8,128)} %bitcast.63, f32[]{:T(128)} %constant.47.clone.1), dimensions={0}, to_apply=%region_0.0 | reduce | flops 5959680 | bytes 27017220 | tf_op jit(solution)/shard_map/reduce_sum | solution.py:25
  160.7 0.1 copy.20
  160.8 0.1 copy.11
  160.9 5.8 %cholesky.74 = f32[64,64]{1,0:T(8,128)S(1)} custom-call(f32[64,64]{1,0:T(8,128)S(1)} %fusion.44), custom_call_target="Cholesky" | custom-call | tf_op jit(solution)/shard_map/jit(cholesky)/cholesky | solution.py:12
  166.8 0.6 compare_reduce_fusion.3
  167.5 0.7 fusion.23
  168.1 4.9 %custom-call.14 = f32[1,64,64]{1,2,0:T(8,128)S(1)} custom-call(f32[1,64,64]{2,1,0:T(8,128)S(1)} %fusion.23), custom_call_target="InvertDiagBlocksLowerTriangular" | custom-call | tf_op jit(solution)/shard_map/jit(_cho_solve)/triangular_solve | solution.py:13
  173.0 1.5 fusion.17
  174.5 1.5 fusion.41
  176.0 1.4 fusion.56
  177.4 9.2 %fusion.4 = f32[64,1024]{1,0:T(8,128)} fusion(bf16[1024,6144]{1,0:T(8,128)(2,1)} %param.7, f32[64,6144]{1,0:T(8,128)S(1)} %fusion.41), kind=kOutput, calls=%fused_computation.4 | convolution fusion | flops 811991040 | bytes 14417920 | tf_op jit(solution)/shard_map/dot_general | solution.py:30
  186.6 8.3 %psum.14 = f32[64,64]{0,1:T(8,128)S(1)} all-reduce(f32[64,64]{0,1:T(8,128)S(1)} %fusion.56), channel_id=1, replica_groups=mesh['samp'=16,'var'=2] {'var'}, use_global_device_ids=true, to_apply=%region_3.6 | all-reduce | flops 4096 | bytes 32768 | tf_op jit(solution)/shard_map/psum | solution.py:35
  194.9 0.0 reduce-scatter.3.cloned.1.call-update
  194.9 0.2 all-gather.7.cloned.1.call-start
  195.2 0.1 copy.13
  195.3 5.8 %cholesky.85 = f32[64,64]{1,0:T(8,128)S(1)} custom-call(f32[64,64]{1,0:T(8,128)S(1)} %fusion.40), custom_call_target="Cholesky" | custom-call | tf_op jit(solution)/shard_map/jit(cholesky)/cholesky | solution.py:12
  201.2 0.6 compare_reduce_fusion.2
  201.8 0.7 fusion.24
  202.5 4.9 %custom-call.15 = f32[1,64,64]{1,2,0:T(8,128)S(1)} custom-call(f32[1,64,64]{2,1,0:T(8,128)S(1)} %fusion.24), custom_call_target="InvertDiagBlocksLowerTriangular" | custom-call | tf_op jit(solution)/shard_map/jit(_cho_solve)/triangular_solve | solution.py:13
  207.4 0.0 reduce-scatter.3.cloned.1.call-done
  207.4 1.2 fusion.38
  208.6 0.3 fusion.36
  208.9 5.6 %all_gather.20 = f32[64,1024]{1,0:T(8,128)S(1)} all-gather(f32[64,512]{1,0:T(8,128)S(1)} %fusion.36), channel_id=1, replica_groups=mesh['samp'=16,'var'=2] {'var'}, dimensions={1}, use_global_device_ids=true | all-gather | bytes 393216 | tf_op jit(solution)/shard_map/all_gather | solution.py:37
  214.5 0.4 fusion.57
  214.9 7.0 %fusion.2 = f32[64,6144]{1,0:T(8,128)S(1)} fusion(bf16[1024,6144]{1,0:T(8,128)(2,1)} %param.7, f32[64,1024]{1,0:T(8,128)S(1)} %all_gather.20), kind=kOutput, calls=%fused_computation.2 | convolution fusion | flops 811663360 | bytes 14417920 | tf_op jit(solution)/shard_map/dot_general | solution.py:22
  221.9 1.3 pad_maximum_fusion.1
  223.2 0.0 all-gather.7.cloned.1.call-update
  223.3 0.0 reduce-scatter.5.cloned.1.call-start
  223.3 130.2 %all-gather.7.cloned.1.call-done = f32[1024,6208]{1,0:T(8,128)} async-done(((f32[64,6208]{1,0:T(8,128)}), f32[1024,6208]{1,0:T(8,128)}) %all-gather.7.cloned.1.call-update) | async-done | bytes 25427984 | tf_op jit(solution)/shard_map/all_gather | solution.py:26
  353.5 9.7 %reduce_sum.19 = f32[64,6208]{1,0:T(8,128)S(1)} reduce(f32[16,64,6208]{2,1,0:T(8,128)} %bitcast.62, f32[]{:T(128)} %constant.47.clone.1), dimensions={0}, to_apply=%region_5.0 | reduce | flops 5959680 | bytes 27017220 | tf_op jit(solution)/shard_map/reduce_sum | solution.py:25
  363.2 0.1 copy.21
  363.3 0.1 copy.15
  363.4 5.8 %cholesky.96 = f32[64,64]{1,0:T(8,128)S(1)} custom-call(f32[64,64]{1,0:T(8,128)S(1)} %fusion.35), custom_call_target="Cholesky" | custom-call | tf_op jit(solution)/shard_map/jit(cholesky)/cholesky | solution.py:12
  369.3 0.6 compare_reduce_fusion.1
  370.0 0.7 fusion.25
  370.6 4.9 %custom-call.16 = f32[1,64,64]{1,2,0:T(8,128)S(1)} custom-call(f32[1,64,64]{2,1,0:T(8,128)S(1)} %fusion.25), custom_call_target="InvertDiagBlocksLowerTriangular" | custom-call | tf_op jit(solution)/shard_map/jit(_cho_solve)/triangular_solve | solution.py:13
  375.5 1.5 fusion.15
  377.0 1.5 fusion.32
  378.5 0.0 copy-start
  378.5 1.4 fusion.58
  379.9 0.0 copy-done
  379.9 9.2 %fusion = f32[64,1024]{1,0:T(8,128)} fusion(bf16[1024,6144]{1,0:T(8,128)(2,1)} %param.7, f32[64,6144]{1,0:T(8,128)S(1)} %fusion.32), kind=kOutput, calls=%fused_computation | convolution fusion | flops 811991040 | bytes 14417920 | tf_op jit(solution)/shard_map/dot_general | solution.py:30
  389.1 8.3 %psum.15 = f32[64,64]{0,1:T(8,128)S(1)} all-reduce(f32[64,64]{0,1:T(8,128)S(1)} %fusion.58), channel_id=1, replica_groups=mesh['samp'=16,'var'=2] {'var'}, use_global_device_ids=true, to_apply=%region_6.10 | all-reduce | flops 4096 | bytes 32768 | tf_op jit(solution)/shard_map/psum | solution.py:35
  397.5 0.1 copy.17
  397.5 0.0 reduce-scatter.5.cloned.1.call-update
  397.6 5.8 %cholesky.107 = f32[64,64]{1,0:T(8,128)S(1)} custom-call(f32[64,64]{1,0:T(8,128)S(1)} %fusion.31), custom_call_target="Cholesky" | custom-call | tf_op jit(solution)/shard_map/jit(cholesky)/cholesky | solution.py:12
  403.5 0.6 compare_reduce_fusion
  404.1 0.6 fusion.26
  404.7 4.9 %custom-call.17 = f32[1,64,64]{1,2,0:T(8,128)S(1)} custom-call(f32[1,64,64]{2,1,0:T(8,128)S(1)} %fusion.26), custom_call_target="InvertDiagBlocksLowerTriangular" | custom-call | tf_op jit(solution)/shard_map/jit(_cho_solve)/triangular_solve | solution.py:13
  409.6 0.0 reduce-scatter.5.cloned.1.call-done
  409.6 1.2 fusion.29
  410.8 0.3 fusion.27
  411.1 5.6 %all_gather.23 = f32[64,1024]{1,0:T(8,128)S(1)} all-gather(f32[64,512]{1,0:T(8,128)S(1)} %fusion.27), channel_id=1, replica_groups=mesh['samp'=16,'var'=2] {'var'}, dimensions={1}, use_global_device_ids=true | all-gather | bytes 393216 | tf_op jit(solution)/shard_map/all_gather | solution.py:37
  416.7 0.7 copy.23
  (14 shorter events, 0.2 us)
Async XLA Ops:
  7.2 143.8 %all-gather.5.cloned.1.call-start = ((), (), s32[]{:S(2)}) async-start(), calls=%async_computation.4 | async-start | bytes 27295744 | tf_op jit(solution)/shard_map/all_gather | solution.py:26
  17.1 190.3 %reduce-scatter.3.cloned.1.call-start = ((), (), s32[]{:S(2)}) async-start(), calls=%async_computation.2 | async-start | bytes 393216 | tf_op jit(solution)/shard_map/reduce_scatter | solution.py:34
  194.9 158.6 %all-gather.7.cloned.1.call-start = ((), (), s32[]{:S(2)}) async-start(), calls=%async_computation.5 | async-start | bytes 27295744 | tf_op jit(solution)/shard_map/all_gather | solution.py:26
  223.3 186.3 %reduce-scatter.5.cloned.1.call-start = ((), (), s32[]{:S(2)}) async-start(), calls=%async_computation.3 | async-start | bytes 393216 | tf_op jit(solution)/shard_map/reduce_scatter | solution.py:34
  378.5 1.4 copy-start
Sparse Core Ops, SparseCore 0:
  17.3 133.6 all-gather.4
  195.1 11.0 reduce-scatter.2
  223.4 130.0 all-gather.6
  397.7 10.9 reduce-scatter.4
